TPU v7x, 32 devices: a whole 2x2x4 slice. The times are simulated.
32 devices in a mesh: dp: 32 (over z, y, x, core).
Axes of the slice: x: 2, y: 2, z: 4, core: 2. Of those that a mesh axis runs over, the one named last changes fastest.
Arguments:
- hidden_in: bfloat16 [4096, 640], P('dp'), may hold values from -6 to 6
- cotangent: bfloat16 [4096, 640], P('dp'), may hold values from -6 to 6
- params: float32 [5573632], P('dp'), may hold values from -4 to 4
- moment_one: float32 [5573632], P('dp'), may hold values from -6 to 6
- moment_two: float32 [5573632], P('dp'), may hold values from 0.02 to 0.5
- seq_lengths: int32 [64], replicated, may hold values from 0 to 128, as said below
- seq_owner: int32 [64], replicated, may hold values from 0 to 31, as said below
Outputs:
- block_out: bfloat16 [4096, 640], P('dp')
- grad_in: float32 [4096, 640], P('dp')
- grad_flat: float32 [5573632], P('dp')
- params_new: float32 [5573632], P('dp')
- moment_one_new: float32 [5573632], P('dp')
- moment_two_new: float32 [5573632], P('dp')
Inputs may be any that keep to these rules, and one draw needn't show every extreme that they name: `seq_lengths`: sequences 2j and 2j + 1 go to the same device; on each device their lengths sum to 1 to 128, and sequence 2j has a token or more; one sequence has exactly 128 tokens and its partner has none; other sequences 2j + 1 may have none too. `seq_owner`: each device holds exactly the two sequences 2j and 2j + 1 for one j.
All inputs are finite; a program needn't handle non-finite values.
Results may differ from a plain program's by a relative error of at most 0.012.
The roundings to bfloat16 on the way count: a program that leaves them out, or rounds other values in their place, can miss the bound.
Values may be sent and summed in bfloat16 or wider, within the bound.
No kernel may reach another device: no remote copies, remote signals or barrier semaphores. Data moves between devices by JAX's collectives and lax.ppermute only.
A program may use at most 128 MiB of HBM per device.

v0:
```python
import jax
import jax.numpy as jnp
from jax import lax
from jax.sharding import PartitionSpec as P

D = 640
FF = 2048
HD = 256
HQ = 1024
CAP = 128
WINDOW = 64
STEP = 3
G1LEN = 1638400
G2LEN = 3932160


def rms_scale(values, gain_vec):
    return (
        values
        * lax.rsqrt(jnp.mean(values * values, axis=-1, keepdims=True) + 1e-06)
        * (1.0 + gain_vec)
    )


def rotate(values, cos_tab, sin_tab):
    half_dim = values.shape[-1] // 2
    lower_half = values[..., :half_dim]
    upper_half = values[..., half_dim:]
    return jnp.concatenate(
        [lower_half * cos_tab - upper_half * sin_tab, upper_half * cos_tab + lower_half * sin_tab],
        axis=-1,
    )


def query_key(query_raw, key_raw, gain_query, gain_key, cos_tab, sin_tab):
    per_head = query_raw.reshape(query_raw.shape[0], -1, HD).transpose(1, 0, 2)
    rot_query = rotate(rms_scale(per_head, gain_query), cos_tab, sin_tab) * HD ** (-0.5)
    rot_key = rotate(rms_scale(key_raw, gain_key), cos_tab, sin_tab)
    return (rot_query, rot_key)


def gated_gelu(gate_proj, up_proj):
    return jax.nn.gelu(gate_proj, approximate=True) * up_proj


def outer_sum(left_side, right_side):
    return lax.dot_general(
        left_side, right_side, (((0,), (0,)), ((), ())), preferred_element_type=jnp.float32
    )


def times_transposed(rows_in, matrix):
    return lax.dot_general(
        rows_in, matrix, (((1,), (1,)), ((), ())), preferred_element_type=jnp.float32
    )


def slot_setup(seq_lengths, seq_owner, device):
    mine_mask = seq_owner == device
    own_lengths = jnp.where(mine_mask, seq_lengths, 0)
    seq_ends = jnp.cumsum(own_lengths, dtype=jnp.int32)
    seq_begins = seq_ends - own_lengths
    slot_index = jnp.arange(CAP, dtype=jnp.int32)
    column = slot_index[:, None]
    inside_mask = (
        mine_mask[None, :] & (seq_begins[None, :] <= column) & (column < seq_ends[None, :])
    )
    live_mask = jnp.any(inside_mask, axis=1)
    seq_label = jnp.sum(
        (mine_mask[None, :] & (seq_ends[None, :] <= column)).astype(jnp.int32),
        axis=1,
        dtype=jnp.int32,
    )
    position = jnp.sum(
        jnp.where(inside_mask, column - seq_begins[None, :], 0), axis=1, dtype=jnp.int32
    )
    row_slot = slot_index[:, None]
    col_slot = slot_index[None, :]
    allowed = live_mask[:, None] & live_mask[None, :] & (
        seq_label[:, None] == seq_label[None, :]
    ) & (col_slot <= row_slot) & (row_slot - col_slot < WINDOW) | (row_slot == col_slot)
    half_dim = HD // 2
    frequency = 10000.0 ** (-2.0 * jnp.arange(half_dim, dtype=jnp.float32) / HD)
    angles = position.astype(jnp.float32)[:, None] * frequency[None, :]
    return (live_mask.astype(jnp.float32), allowed, jnp.cos(angles), jnp.sin(angles))


def attend(rot_query, rot_key, value_vec, allowed):
    num_heads = rot_query.shape[0]
    num_slots = rot_key.shape[0]
    flat_query = rot_query.reshape(num_heads * num_slots, HD)
    scores = lax.dot_general(
        flat_query, rot_key, (((1,), (1,)), ((), ())), preferred_element_type=jnp.float32
    )
    scores = jnp.where(allowed[None], scores.reshape(num_heads, num_slots, num_slots), -1e30)
    row_max = jnp.max(scores, axis=-1, keepdims=True)
    raised = jnp.exp(scores - row_max)
    summed = jnp.sum(raised, axis=-1, keepdims=True)
    log_total = row_max + jnp.log(summed)
    attn_prob = (raised / summed).astype(jnp.bfloat16)
    context = jnp.dot(
        attn_prob.reshape(num_heads * num_slots, num_slots),
        value_vec,
        preferred_element_type=jnp.float32,
    )
    context = (
        context.reshape(num_heads, num_slots, HD)
        .transpose(1, 0, 2)
        .reshape(num_slots, num_heads * HD)
    )
    return (context.astype(jnp.bfloat16), log_total)


def attend_back(rot_query, rot_key, value_vec, allowed, log_total, context, delta_context):
    num_heads = rot_query.shape[0]
    num_slots = rot_key.shape[0]
    head_delta = delta_context.reshape(num_slots, num_heads, HD).transpose(1, 0, 2).reshape(-1, HD)
    head_context = context.reshape(num_slots, num_heads, HD).transpose(1, 0, 2).reshape(-1, HD)
    row_dot = jnp.sum(
        head_delta.astype(jnp.float32) * head_context.astype(jnp.float32), axis=-1, keepdims=True
    )
    flat_query = rot_query.reshape(-1, HD)
    scores = lax.dot_general(
        flat_query, rot_key, (((1,), (1,)), ((), ())), preferred_element_type=jnp.float32
    )
    scores = jnp.where(allowed[None], scores.reshape(num_heads, num_slots, num_slots), -1e30)
    prob_exact = jnp.exp(scores - log_total).reshape(-1, num_slots)
    delta_value = lax.dot_general(
        prob_exact.astype(jnp.bfloat16),
        head_delta,
        (((0,), (0,)), ((), ())),
        preferred_element_type=jnp.float32,
    )
    delta_prob = lax.dot_general(
        head_delta, value_vec, (((1,), (1,)), ((), ())), preferred_element_type=jnp.float32
    )
    delta_score = (prob_exact * (delta_prob - row_dot)).astype(jnp.bfloat16)
    delta_query = jnp.dot(delta_score, rot_key, preferred_element_type=jnp.float32).reshape(
        num_heads, num_slots, HD
    )
    delta_key = lax.dot_general(
        delta_score, flat_query, (((0,), (0,)), ((), ())), preferred_element_type=jnp.float32
    )
    return (delta_query, delta_key, delta_value.astype(jnp.bfloat16))


def flat_table(arrays, devices):
    return jnp.concatenate([member.reshape(-1) for member in arrays]).reshape(devices, -1)


def unpack_weights(attn_flat, ffn_flat, gain_flat):
    cut_query = D * HQ
    cut_key = cut_query + D * HD
    cut_value = cut_key + D * HD
    query_weight = attn_flat[:cut_query].reshape(D, HQ)
    key_weight = attn_flat[cut_query:cut_key].reshape(D, HD)
    value_weight = attn_flat[cut_key:cut_value].reshape(D, HD)
    out_weight = attn_flat[cut_value:].reshape(HQ, D)
    cut_gate = D * FF
    gate_weight = ffn_flat[:cut_gate].reshape(D, FF)
    up_weight = ffn_flat[cut_gate : 2 * cut_gate].reshape(D, FF)
    down_weight = ffn_flat[2 * cut_gate :].reshape(FF, D)
    gains = gain_flat.astype(jnp.float32)
    gain_set = (
        gains[:D],
        gains[D : D + HD],
        gains[D + HD : D + 2 * HD],
        gains[D + 2 * HD : 2 * D + 2 * HD],
        gains[2 * D + 2 * HD : 3 * D + 2 * HD],
        gains[3 * D + 2 * HD :],
    )
    return (
        query_weight,
        key_weight,
        value_weight,
        out_weight,
        gate_weight,
        up_weight,
        down_weight,
        gain_set,
    )


def forward_pass(input_rows, weights, allowed, cos_tab, sin_tab):
    (
        query_weight,
        key_weight,
        value_weight,
        out_weight,
        gate_weight,
        up_weight,
        down_weight,
        gain_set,
    ) = weights
    gain_in, gain_query, gain_key, gain_post, gain_mid, gain_last = gain_set
    resid_in = input_rows.astype(jnp.float32)
    normed_in = rms_scale(resid_in, gain_in).astype(jnp.bfloat16)
    query_raw = jnp.dot(normed_in, query_weight, preferred_element_type=jnp.float32)
    key_raw = jnp.dot(normed_in, key_weight, preferred_element_type=jnp.float32)
    value_vec = jnp.dot(normed_in, value_weight, preferred_element_type=jnp.float32).astype(
        jnp.bfloat16
    )
    rot_query, rot_key = query_key(query_raw, key_raw, gain_query, gain_key, cos_tab, sin_tab)
    rot_query = rot_query.astype(jnp.bfloat16)
    rot_key = rot_key.astype(jnp.bfloat16)
    context, log_total = attend(rot_query, rot_key, value_vec, allowed)
    attn_out = jnp.dot(context, out_weight, preferred_element_type=jnp.float32)
    mid_stream = resid_in + rms_scale(attn_out, gain_post)
    normed_mid = rms_scale(mid_stream, gain_mid).astype(jnp.bfloat16)
    gate_proj = jnp.dot(normed_mid, gate_weight, preferred_element_type=jnp.float32)
    up_proj = jnp.dot(normed_mid, up_weight, preferred_element_type=jnp.float32)
    hidden = gated_gelu(gate_proj, up_proj).astype(jnp.bfloat16)
    ffn_out = jnp.dot(hidden, down_weight, preferred_element_type=jnp.float32)
    block_out = (mid_stream + rms_scale(ffn_out, gain_last)).astype(jnp.bfloat16)
    saved = (
        resid_in,
        normed_in,
        query_raw,
        key_raw,
        value_vec,
        rot_query,
        rot_key,
        context,
        log_total,
        attn_out,
        mid_stream,
        normed_mid,
        gate_proj,
        up_proj,
        hidden,
        ffn_out,
    )
    return (block_out, saved)


def ffn_backward(cot_rows, live_mask, weights, saved):
    gate_weight, up_weight, down_weight, gain_set = (weights[4], weights[5], weights[6], weights[7])
    gain_mid, gain_last = (gain_set[4], gain_set[5])
    mid_stream, normed_mid, gate_proj, up_proj, hidden, ffn_out = saved[10:]
    delta_out = cot_rows.astype(jnp.float32) * live_mask[:, None]
    unused, pullback = jax.vjp(rms_scale, ffn_out, gain_last)
    delta_ffn, gain_last_grad = pullback(delta_out)
    delta_ffn = delta_ffn.astype(jnp.bfloat16)
    down_grad = outer_sum(hidden, delta_ffn)
    delta_hidden = times_transposed(delta_ffn, down_weight)
    unused, pullback = jax.vjp(gated_gelu, gate_proj, up_proj)
    delta_gate, delta_up = pullback(delta_hidden)
    delta_gate = delta_gate.astype(jnp.bfloat16)
    delta_up = delta_up.astype(jnp.bfloat16)
    gate_grad = outer_sum(normed_mid, delta_gate)
    up_grad = outer_sum(normed_mid, delta_up)
    delta_normed = times_transposed(delta_gate, gate_weight) + times_transposed(delta_up, up_weight)
    unused, pullback = jax.vjp(rms_scale, mid_stream, gain_mid)
    delta_part, gain_mid_grad = pullback(delta_normed)
    delta_mid = delta_out + delta_part
    return (delta_mid, (gate_grad, up_grad, down_grad), (gain_mid_grad, gain_last_grad))


def attn_backward(delta_mid, weights, saved, allowed, cos_tab, sin_tab):
    query_weight, key_weight, value_weight, out_weight = weights[:4]
    gain_in, gain_query, gain_key, gain_post = weights[7][:4]
    (
        resid_in,
        normed_in,
        query_raw,
        key_raw,
        value_vec,
        rot_query,
        rot_key,
        context,
        log_total,
        attn_out,
    ) = saved[:10]
    unused, pullback = jax.vjp(rms_scale, attn_out, gain_post)
    delta_attn, gain_post_grad = pullback(delta_mid)
    delta_attn = delta_attn.astype(jnp.bfloat16)
    out_grad = outer_sum(context, delta_attn)
    delta_context = times_transposed(delta_attn, out_weight).astype(jnp.bfloat16)
    delta_query, delta_key, delta_value = attend_back(
        rot_query, rot_key, value_vec, allowed, log_total, context, delta_context
    )

    def rope_map(raw_query, raw_key, query_gain, key_gain):
        return query_key(raw_query, raw_key, query_gain, key_gain, cos_tab, sin_tab)

    unused, pullback = jax.vjp(rope_map, query_raw, key_raw, gain_query, gain_key)
    delta_qraw, delta_kraw, gain_query_grad, gain_key_grad = pullback((delta_query, delta_key))
    delta_qraw = delta_qraw.astype(jnp.bfloat16)
    delta_kraw = delta_kraw.astype(jnp.bfloat16)
    query_grad = outer_sum(normed_in, delta_qraw)
    key_grad = outer_sum(normed_in, delta_kraw)
    value_grad = outer_sum(normed_in, delta_value)
    delta_in = (
        times_transposed(delta_qraw, query_weight)
        + times_transposed(delta_kraw, key_weight)
        + times_transposed(delta_value, value_weight)
    )
    unused, pullback = jax.vjp(rms_scale, resid_in, gain_in)
    delta_part, gain_in_grad = pullback(delta_in)
    grad_in = delta_mid + delta_part
    return (
        grad_in,
        (query_grad, key_grad, value_grad, out_grad),
        (gain_in_grad, gain_query_grad, gain_key_grad, gain_post_grad),
    )


def adam_update(weight_shard, gradient, moment_one, moment_two):
    moment_one = 0.9 * moment_one + 0.1 * gradient
    moment_two = 0.999 * moment_two + 0.001 * gradient * gradient
    fix_one = 1.0 - 0.9**STEP
    fix_two = 1.0 - 0.999**STEP
    weight_shard = weight_shard - 0.02 * (
        moment_one / fix_one / (jnp.sqrt(moment_two / fix_two) + 1e-08) + 0.1 * weight_shard
    )
    return (weight_shard, moment_one, moment_two)


def per_device(hidden_in, cotangent, params, moment_one, moment_two, seq_lengths, seq_owner):
    devices = lax.axis_size("dp")
    attn_len = G1LEN // devices
    ffn_len = G2LEN // devices
    rounded = params.astype(jnp.bfloat16)
    attn_flat, ffn_flat, gain_flat = (
        lax.all_gather(rounded[:attn_len], "dp", axis=0, tiled=True),
        lax.all_gather(rounded[attn_len : attn_len + ffn_len], "dp", axis=0, tiled=True),
        lax.all_gather(rounded[attn_len + ffn_len :], "dp", axis=0, tiled=True),
    )
    weights = unpack_weights(attn_flat, ffn_flat, gain_flat)
    device = lax.axis_index("dp")
    live_mask, allowed, cos_tab, sin_tab = slot_setup(seq_lengths, seq_owner, device)
    block_out, saved = forward_pass(hidden_in, weights, allowed, cos_tab, sin_tab)
    delta_mid, ffn_grads, late_gains = ffn_backward(cotangent, live_mask, weights, saved)
    ffn_group = flat_table(ffn_grads, devices)
    grad_in, attn_grads, early_gains = attn_backward(
        delta_mid, weights, saved, allowed, cos_tab, sin_tab
    )
    attn_group = flat_table(attn_grads, devices)
    gain_group = flat_table(early_gains + late_gains, devices)
    attn_shard, ffn_shard, gain_shard = (
        lax.psum_scatter(attn_group, "dp", scatter_dimension=0, tiled=True),
        lax.psum_scatter(ffn_group, "dp", scatter_dimension=0, tiled=True),
        lax.psum_scatter(gain_group, "dp", scatter_dimension=0, tiled=True),
    )
    grad_shard = jnp.concatenate(
        [attn_shard.reshape(-1), ffn_shard.reshape(-1), gain_shard.reshape(-1)]
    )
    params_new, moment_one_new, moment_two_new = adam_update(
        params, grad_shard, moment_one, moment_two
    )
    return (block_out, grad_in, grad_shard, params_new, moment_one_new, moment_two_new)


def solution(mesh):
    in_specs = (P("dp", None), P("dp", None), P("dp"), P("dp"), P("dp"), P(), P())
    out_specs = (P("dp", None), P("dp", None), P("dp"), P("dp"), P("dp"), P("dp"))
    return jax.shard_map(
        per_device, mesh=mesh, in_specs=in_specs, out_specs=out_specs, check_vma=False
    )
```

profile of v0, /device:TPU:0, one launch (start us, length us, event | category | flops | bytes accessed | tf_op | source)
XLA Modules:
  0.0 640.0 jit_solution(17678911759446597382)
XLA Ops:
  7.2 1.1 convert_element_type.113
  12.6 42.2 %all-reduce.4 = bf16[3072]{0:T(1024)(128)(2,1)S(1)} all-reduce(bf16[3072]{0:T(1024)(128)(2,1)S(1)} %dynamic-update-slice), channel_id=1, replica_groups=mesh['dp'=32] {'dp'}, use_global_device_ids=true, to_apply=%add.4 | all-reduce | flops 3072 | bytes 12288
  55.4 1.0 fusion.22
  57.7 16.1 %all-gather.3.cloned.1.call-done = bf16[1638400]{0:T(1024)(128)(2,1)} async-done(((bf16[51200]{0:T(1024)(128)(2,1)}), bf16[1638400]{0:T(1024)(128)(2,1)}) %all-gather.3.cloned.1.call-update) | async-done | bytes 3276816 | tf_op jit(solution)/shard_map/all_gather | solution.py:325
  73.7 3.0 fusion.90
  76.7 1.0 slice.146
  77.7 1.6 fusion.91
  80.2 2.5 slice.134
  82.8 1.6 copy.30
  84.8 2.0 multiply_reduce_fusion.3
  91.8 58.5 %all-gather.5.cloned.1.call-done = bf16[3932160]{0:T(1024)(128)(2,1)} async-done(((bf16[122880]{0:T(1024)(128)(2,1)}), bf16[3932160]{0:T(1024)(128)(2,1)}) %all-gather.5.cloned.1.call-update) | async-done | bytes 7864336 | tf_op jit(solution)/shard_map/all_gather | solution.py:326
  150.2 5.0 fusion.89
  155.3 3.1 slice.155
  158.4 3.8 slice.153
  162.2 5.2 slice.151
  167.4 2.3 fusion.93
  172.2 1.5 multiply_reduce_fusion.4
  173.6 1.4 multiply_convert_fusion
  176.4 1.7 multiply_reduce_fusion.5
  179.1 1.3 convolution_convert_fusion
  180.8 3.3 fusion.76
  184.1 3.1 convolution_bitcast_fusion
  187.2 3.2 convolution_bitcast_fusion.1
  190.4 1.8 copy.32
  192.3 1.8 copy.33
  194.1 1.2 multiply_reduce_fusion.2
  195.3 1.9 fusion.2
  197.2 1.3 fusion.1
  198.5 1.0 convolution_multiply_fusion
  199.8 1.0 fusion.50
  204.1 1.8 copy.34
  205.9 1.2 convolution_bitcast_fusion.3
  207.8 1.2 copy.38
  208.9 1.7 reshape.478
  210.6 1.6 convolution_bitcast_fusion.2
  214.1 8.2 %pad_maximum_fusion.1 = f32[1638400]{0:T(1024)} fusion(f32[655360]{0:T(1024)S(1)} %copy-done.6, f32[163840]{0:T(1024)S(1)} %bitcast.107, f32[163840]{0:T(1024)S(1)} %bitcast.108, f32[655360]{0:T(1024)S(1)} %bitcast.104), kind=kLoop, calls=%fused_computation.1 | loop fusion | flops 4915200 | bytes 13107200 | tf_op jit(solution)/shard_map/concatenate | solution.py:148
  222.3 6.3 reshape.479
  228.6 6.6 %reshape.483 = f32[1310720]{0:T(1024)} reshape(f32[2048,640]{1,0:T(8,128)} %fusion.76) | data formatting | bytes 10485760 | tf_op jit(solution)/shard_map/reshape | solution.py:148
  235.2 3.9 copy.41
  239.1 1.2 copy.40
  240.7 17.2 %pad_maximum_fusion = f32[3932160]{0:T(1024)} fusion(f32[1310720]{0:T(1024)S(1)} %bitcast.100, f32[1310720]{0:T(1024)S(1)} %bitcast.101, f32[1310720]{0:T(1024)S(1)} %bitcast.102), kind=kLoop, calls=%fused_computation | loop fusion | flops 7864320 | bytes 31457280 | tf_op jit(solution)/shard_map/concatenate | solution.py:148
  257.9 11.7 %reshape.484 = f32[32,122880]{1,0:T(8,128)} reshape(f32[3932160]{0:T(1024)} %pad_maximum_fusion) | data formatting | bytes 31457280 | tf_op jit(solution)/shard_map/reshape | solution.py:148
  269.7 1.2 copy-done.2
  272.3 41.1 %all-reduce.7 = f32[32,96]{1,0:T(8,128)S(1)} all-reduce(f32[32,96]{1,0:T(8,128)S(1)} %reshape.486), channel_id=4, replica_groups=mesh['dp'=32] {'dp'}, use_global_device_ids=true, to_apply=%region_27.28.clone | all-reduce | flops 3072 | bytes 24576
  314.3 312.3 %all-reduce.11.cloned.1.call-done = (f32[32,122880]{1,0:T(8,128)}, f32[32,51200]{1,0:T(8,128)}) async-done(((f32[32,122880]{1,0:T(8,128)}, f32[32,51200]{1,0:T(8,128)}), (f32[32,122880]{1,0:T(8,128)}, f32[32,51200]{1,0:T(8,128)})) %all-reduce.11.cloned.1.call-update) | async-done | bytes 22282256
  626.6 2.5 constant_dynamic-slice_fusion.1
  629.1 1.6 constant_dynamic-slice_fusion.2
  630.7 2.8 multiply_subtract_fusion
  (231 shorter events, 25.8 us)
Async XLA Ops:
  7.2 66.6 %all-gather.3.cloned.1.call-start = ((), (), s32[]{:S(2)}) async-start(), calls=%async_computation | async-start | bytes 3379200 | tf_op jit(solution)/shard_map/all_gather | solution.py:325
  9.0 141.2 %all-gather.5.cloned.1.call-start = ((), (), s32[]{:S(2)}) async-start(), calls=%async_computation.1 | async-start | bytes 8110080 | tf_op jit(solution)/shard_map/all_gather | solution.py:326
  9.8 616.8 %all-reduce.11.cloned.1.call-start = ((), (), s32[]{:S(2)}) async-start(), calls=%async_computation.2 | async-start | bytes 44564480
  55.4 31.5 %copy-start.46 = (f32[256]{0:T(256)}, f32[256]{0:T(256)S(1)}, u32[]{:S(2)}) copy-start(f32[256]{0:T(256)S(1)} %get-tuple-element.53) | copy-start | bytes 3076
  56.4 31.8 %copy-start.44 = (f32[128]{0:T(128)}, f32[128]{0:T(128)S(1)}, u32[]{:S(2)}) copy-start(f32[128]{0:T(128)S(1)} %fusion.63) | copy-start | bytes 1540
  77.7 11.6 %copy-start.3 = (bf16[1024,640]{1,0:T(8,128)(2,1)}, bf16[1024,640]{1,0:T(8,128)(2,1)S(1)}, u32[]{:S(2)}) copy-start(bf16[1024,640]{1,0:T(8,128)(2,1)S(1)} %slice.146) | copy-start | bytes 3932164
  80.2 4.1 copy-start.20
  80.2 4.1 copy-start.7
  82.8 4.0 copy-start.1
  84.4 2.6 copy-start.61
  84.4 2.6 copy-start.62
  84.4 3.0 copy-start.51
  84.7 2.1 copy-start.69
  84.7 3.2 copy-start.24
  84.7 2.1 copy-start.53
  84.8 3.4 copy-start.22
  86.8 2.0 copy-start.42
  86.8 2.0 copy-start.40
  89.1 2.7 copy-start.30
  89.3 2.5 copy-start.16
  176.4 2.6 copy-start.66
  176.4 2.7 copy-start.4
  178.0 2.3 copy-start.17
  190.4 8.1 %copy-start.37 = (bf16[128,128]{1,0:T(8,128)(2,1)S(1)}, bf16[128,128]{1,0:T(8,128)(2,1)}, u32[]{:S(2)}) copy-start(bf16[128,128]{1,0:T(8,128)(2,1)} %copy-done.36) | copy-start | bytes 98308
  190.4 10.3 %copy-start.25 = (f32[128,256]{1,0:T(8,128)S(1)}, f32[128,256]{1,0:T(8,128)}, u32[]{:S(2)}) copy-start(f32[128,256]{1,0:T(8,128)} %copy-done.24) | copy-start | bytes 393220
  190.4 10.3 %copy-start.47 = (f32[256]{0:T(256)S(1)}, f32[256]{0:T(256)}, u32[]{:S(2)}) copy-start(f32[256]{0:T(256)} %copy-done.46) | copy-start | bytes 3076
  190.4 10.3 %copy-start.54 = (f32[128]{0:T(128)S(1)}, f32[128]{0:T(128)}, u32[]{:S(2)}) copy-start(f32[128]{0:T(128)} %copy-done.53) | copy-start | bytes 1540
  194.1 5.4 copy-start.27
  194.1 5.4 copy-start.29
  194.1 8.7 %copy-start.33 = (f32[128,128]{1,0:T(8,128)S(1)}, f32[128,128]{1,0:T(8,128)}, u32[]{:S(2)}) copy-start(f32[128,128]{1,0:T(8,128)} %copy-done.32) | copy-start | bytes 196612
  194.1 8.8 %copy-start.41 = (f32[4,128]{1,0:T(4,128)S(1)}, f32[4,128]{1,0:T(4,128)}, u32[]{:S(2)}) copy-start(f32[4,128]{1,0:T(4,128)} %copy-done.40) | copy-start | bytes 6148
  194.1 8.8 %copy-start.52 = (f32[256]{0:T(256)S(1)}, f32[256]{0:T(256)}, u32[]{:S(2)}) copy-start(f32[256]{0:T(256)} %get-tuple-element.54) | copy-start | bytes 3076
  197.2 5.9 copy-start.43
  199.7 6.1 copy-start.45
  202.9 4.5 copy-start.35
  228.6 10.5 %slice-start = ((s8[5242880]{0:T(1024)(128)(4,1)}), s8[1048576]{0:T(1024)(128)(4,1)S(1)}, s32[]{:S(2)}) async-start(s8[5242880]{0:T(1024)(128)(4,1)} %bitcast.97), calls=%async_computation.3 | async-start | bytes 2097152
  235.2 3.9 slice-start.1
  235.2 5.1 slice-start.2
  269.6 2.1 copy-start.23
  269.6 2.1 copy-start.34
  269.6 2.5 copy-start.60
  269.6 2.6 copy-start.50
  269.6 2.6 copy-start.49
  269.6 2.6 copy-start.48
  269.6 43.8 %copy-start.64 = (f32[128]{0:T(128)S(1)}, f32[128]{0:T(128)}, u32[]{:S(2)}) copy-start(f32[128]{0:T(128)} %copy-done.63) | copy-start | bytes 1540
  269.6 43.8 %copy-start.13 = (f32[128,640]{1,0:T(8,128)S(1)}, f32[128,640]{1,0:T(8,128)}, u32[]{:S(2)}) copy-start(f32[128,640]{1,0:T(8,128)} %copy-done.12) | copy-start | bytes 983044
  271.4 359.2 %copy-start.14 = (f32[174176]{0:T(1024)S(1)}, f32[174176]{0:T(1024)}, u32[]{:S(2)}) copy-start(f32[174176]{0:T(1024)} %param.9) | copy-start | bytes 2090116
  271.5 359.2 %copy-start.31 = (f32[174176]{0:T(1024)S(1)}, f32[174176]{0:T(1024)}, u32[]{:S(2)}) copy-start(f32[174176]{0:T(1024)} %param.10) | copy-start | bytes 2090116
  (29 other events, 40.9 us)
Sparse Core Ops, SparseCore 0:
  11.4 62.2 all-gather.2
  76.6 73.5 all-gather.4
  269.7 356.8 all-reduce.10
where the time goes:
time: 641 us; the launch traced here: 640 us
  waiting for transfers between devices  387 us (60%)
  blocking collectives  83.3 us (13%)
  local copies, waits for them, and re-layouts  77.9 us (12%)
  other arithmetic  45.4 us (7%)
  matrix products  31.4 us (5%)
  between operations  15 us (2%)
    unnamed x4, waiting for transfers between devices  312 us
    unnamed x2, blocking collectives  83.3 us
    all_gather x1, waiting for transfers between devices, per_device(): lax.all_gather(rounded[attn_len:attn_len + ffn_len], 'dp', axis=0, tiled=...  58.5 us
    concatenate x2, other arithmetic, flat_table(): jnp.concatenate([member.reshape(-1) for member in arrays])  25.4 us
    reshape x3, local copies, waits for them, and re-layouts, flat_table(): jnp.concatenate([member.reshape(-1) for member in arrays])  18.1 us
    unnamed x162, local copies, waits for them, and re-layouts  16.7 us
    all_gather x1, waiting for transfers between devices, per_device(): lax.all_gather(rounded[:attn_len], 'dp', axis=0, tiled=True)  16.1 us
    dot_general x7, matrix products, outer_sum(): lax.dot_general(left_side, right_side, (((0,), (0,)), ((), ())), preferre...  13.2 us
  transfers between devices with their start and end apart: 3, of which 3 were waited for; matrix products, arithmetic and copies ran while one was open for 4% of the time, Pallas kernels for 0%

commit v1 on v0

--- a/solution.py
+++ b/solution.py
@@ -12,6 +12,8 @@
 STEP = 3
 G1LEN = 1638400
 G2LEN = 3932160
+LANE_BLOCK = 1024
+SEND = jnp.bfloat16
 
 
 def rms_scale(values, gain_vec):
@@ -316,35 +318,46 @@
     return (weight_shard, moment_one, moment_two)
 
 
+def padded_length(entries):
+    return -(-entries // LANE_BLOCK) * LANE_BLOCK
+
+
 def per_device(hidden_in, cotangent, params, moment_one, moment_two, seq_lengths, seq_owner):
     devices = lax.axis_size("dp")
     attn_len = G1LEN // devices
     ffn_len = G2LEN // devices
+    gain_len = params.shape[0] - attn_len - ffn_len
+    small_len = attn_len + gain_len
+    pad_len = padded_length(small_len) - small_len
     rounded = params.astype(jnp.bfloat16)
-    attn_flat, ffn_flat, gain_flat = (
-        lax.all_gather(rounded[:attn_len], "dp", axis=0, tiled=True),
-        lax.all_gather(rounded[attn_len : attn_len + ffn_len], "dp", axis=0, tiled=True),
-        lax.all_gather(rounded[attn_len + ffn_len :], "dp", axis=0, tiled=True),
-    )
+    first_part = jnp.concatenate(
+        [rounded[:attn_len], rounded[attn_len + ffn_len :], jnp.zeros((pad_len,), jnp.bfloat16)]
+    )
+    first_table = lax.all_gather(first_part, "dp", axis=0, tiled=True).reshape(devices, -1)
+    attn_flat = first_table[:, :attn_len].reshape(-1)
+    gain_flat = first_table[:, attn_len:small_len].reshape(-1)
+    ffn_flat = lax.all_gather(rounded[attn_len : attn_len + ffn_len], "dp", axis=0, tiled=True)
     weights = unpack_weights(attn_flat, ffn_flat, gain_flat)
     device = lax.axis_index("dp")
     live_mask, allowed, cos_tab, sin_tab = slot_setup(seq_lengths, seq_owner, device)
     block_out, saved = forward_pass(hidden_in, weights, allowed, cos_tab, sin_tab)
     delta_mid, ffn_grads, late_gains = ffn_backward(cotangent, live_mask, weights, saved)
-    ffn_group = flat_table(ffn_grads, devices)
+    ffn_group = jnp.concatenate([member.astype(SEND).reshape(-1) for member in ffn_grads])
+    ffn_shard = lax.psum_scatter(ffn_group, "dp", scatter_dimension=0, tiled=True)
     grad_in, attn_grads, early_gains = attn_backward(
         delta_mid, weights, saved, allowed, cos_tab, sin_tab
     )
-    attn_group = flat_table(attn_grads, devices)
-    gain_group = flat_table(early_gains + late_gains, devices)
-    attn_shard, ffn_shard, gain_shard = (
-        lax.psum_scatter(attn_group, "dp", scatter_dimension=0, tiled=True),
-        lax.psum_scatter(ffn_group, "dp", scatter_dimension=0, tiled=True),
-        lax.psum_scatter(gain_group, "dp", scatter_dimension=0, tiled=True),
-    )
+    attn_group = flat_table([member.astype(SEND) for member in attn_grads], devices)
+    gain_group = flat_table(
+        [member.astype(SEND) for member in early_gains + late_gains], devices
+    )
+    small_group = jnp.concatenate(
+        [attn_group, gain_group, jnp.zeros((devices, pad_len), SEND)], axis=1
+    ).reshape(-1)
+    small_shard = lax.psum_scatter(small_group, "dp", scatter_dimension=0, tiled=True)
     grad_shard = jnp.concatenate(
-        [attn_shard.reshape(-1), ffn_shard.reshape(-1), gain_shard.reshape(-1)]
-    )
+        [small_shard[:attn_len], ffn_shard, small_shard[attn_len:small_len]]
+    ).astype(jnp.float32)
     params_new, moment_one_new, moment_two_new = adam_update(
         params, grad_shard, moment_one, moment_two
     )

time: 641 us -> 531 us (0.83)
  blocking collectives: 83.3 us -> 0 us
  waiting for transfers between devices: 387 us -> 317 us
  other arithmetic: 45.4 us -> 79.6 us
    unnamed x4, waiting for transfers between devices: 312 us -> 215 us
    unnamed x2 -> x0, blocking collectives: 83.3 us -> none
    concatenate x0 -> x1, other arithmetic: none -> 44.6 us  [per_device(): jnp.concatenate([member.astype(SEND).reshape(-1) for member in ffn_grads])]
    all_gather x1, waiting for transfers between devices: 16.1 us -> 56.5 us  [per_device(): lax.all_gather(first_part, 'dp', axis=0, tiled=True).reshape(devices, -1)]
    reshape x3 -> x2, local copies, waits for them, and re-layouts: 18.1 us -> 2.97 us  [flat_table(): jnp.concatenate([member.reshape(-1) for member in arrays])]
    all_gather x1, waiting for transfers between devices: 58.5 us -> 44.9 us  [per_device(): lax.all_gather(rounded[attn_len:attn_len + ffn_len], 'dp', axis=0, tiled=...]
    reshape x1 -> x2, local copies, waits for them, and re-layouts: 0.01 us -> 10.6 us  [the longest x1 5.68 us: per_device(): member.astype(SEND).reshape(-1)]
    concatenate x2 -> x1, other arithmetic: 25.4 us -> 18.3 us  [flat_table(): jnp.concatenate([member.reshape(-1) for member in arrays])]
  transfers between devices with their start and end apart: 3 -> 3, of which waited for: 3 -> 3; matrix products, arithmetic and copies ran while one was open for 4% -> 7% of each run, Pallas kernels for 0% -> 0%
where the time goes in v1:
time: 531 us; the launch traced here: 524 us
  waiting for transfers between devices  317 us (60%)
  other arithmetic  79.6 us (15%)
  local copies, waits for them, and re-layouts  77.5 us (15%)
  matrix products  34.7 us (7%)
  between operations  15.2 us (3%)
    unnamed x4, waiting for transfers between devices  215 us
    all_gather x1, waiting for transfers between devices, per_device(): lax.all_gather(first_part, 'dp', axis=0, tiled=True).reshape(devices, -1)  56.5 us
    all_gather x1, waiting for transfers between devices, per_device(): lax.all_gather(rounded[attn_len:attn_len + ffn_len], 'dp', axis=0, tiled=...  44.9 us
    concatenate x1, other arithmetic, per_device(): jnp.concatenate([member.astype(SEND).reshape(-1) for member in ffn_grads])  44.6 us
    unnamed x178, local copies, waits for them, and re-layouts  18.9 us
    concatenate x1, other arithmetic, flat_table(): jnp.concatenate([member.reshape(-1) for member in arrays])  18.3 us
    dot_general x7, matrix products, times_transposed(): lax.dot_general(rows_in, matrix, (((1,), (1,)), ((), ())), preferred_elem...  11.6 us
    dot_general x7, matrix products, outer_sum(): lax.dot_general(left_side, right_side, (((0,), (0,)), ((), ())), preferre...  11.2 us
  transfers between devices with their start and end apart: 3, of which 3 were waited for; matrix products, arithmetic and copies ran while one was open for 7% of the time, Pallas kernels for 0%

profile of v1, /device:TPU:0, one launch (start us, length us, event | category | flops | bytes accessed | tf_op | source)
XLA Modules:
  0.0 523.8 jit_solution(7832364587390750147)
XLA Ops:
  7.2 1.1 convert_element_type.158
  8.4 2.7 concatenate.33
  15.6 1.0 fusion.32
  17.4 56.5 %all-gather.3.cloned.1.call-done = bf16[1671168]{0:T(1024)(128)(2,1)} async-done(((bf16[52224]{0:T(1024)(128)(2,1)}), bf16[1671168]{0:T(1024)(128)(2,1)}) %all-gather.3.cloned.1.call-update) | async-done | bytes 3342352 | tf_op jit(solution)/shard_map/all_gather | solution.py:336
  73.8 4.9 reshape.446
  78.7 2.1 slice.146
  80.9 3.0 slice.122
  83.8 3.0 slice.128
  86.8 5.9 %slice.117 = bf16[1600,1024]{1,0:T(8,128)(2,1)} reshape(bf16[32,51200]{1,0:T(8,128)(2,1)S(1)} %slice.146) | data formatting | bytes 6553600 | tf_op jit(solution)/shard_map/slice | solution.py:157
  93.5 1.5 slice_bitcast_fusion
  95.8 1.3 multiply_reduce_fusion.15
  100.3 1.2 convolution_convert_fusion.9
  102.1 1.9 multiply_reduce_fusion.12
  106.0 44.9 %all-gather.5.cloned.1.call-done = bf16[3932160]{0:T(1024)(128)(2,1)} async-done(((bf16[122880]{0:T(1024)(128)(2,1)}), bf16[3932160]{0:T(1024)(128)(2,1)}) %all-gather.5.cloned.1.call-update) | async-done | bytes 7864336 | tf_op jit(solution)/shard_map/all_gather | solution.py:339
  150.8 5.2 fusion.101
  156.0 3.1 slice.138
  159.1 3.8 slice.136
  163.0 5.6 %slice.134 = bf16[640,2048]{1,0:T(8,128)(2,1)} reshape(bf16[1310720]{0:T(1024)(128)(2,1)} %get-tuple-element.33) | data formatting | bytes 5242880 | tf_op jit(solution)/shard_map/slice | solution.py:162
  168.6 2.3 fusion.103
  173.4 1.5 multiply_reduce_fusion.4
  174.9 1.4 multiply_convert_fusion
  176.7 0.9 fusion.104
  177.6 1.7 multiply_reduce_fusion.5
  181.0 2.6 convolution_convert_fusion.7
  184.1 1.1 copy.32
  186.4 1.1 fusion.11
  187.8 1.5 multiply_reduce_fusion
  190.5 1.9 fusion.9
  192.4 1.6 fusion.2
  194.1 3.5 convolution_convert_fusion
  197.6 2.4 fusion.1
  200.1 2.4 fusion
  203.9 1.0 copy.39
  205.2 1.0 copy.38
  206.2 1.2 convolution_add_fusion.1
  207.4 2.0 fusion.27
  210.7 2.0 reshape.453
  213.1 0.9 copy-done.10
  214.1 18.3 %pad_maximum_fusion.1 = bf16[1638400]{0:T(1024)(128)(2,1)S(1)} fusion(bf16[655360]{0:T(1024)(128)(2,1)S(1)} %copy-done.10, bf16[163840]{0:T(1024)(128)(2,1)S(1)} %bitcast.100, bf16[163840]{0:T(1024)(128)(2,1)S(1)} %bitcast.101, bf16[655360]{0:T(1024)(128)(2,1)S(1)} %bitcast.94), kind=kLoop, calls=%fused_computation.1 | loop fusion | flops 13107200 | bytes 6553600 | tf_op jit(solution)/shard_map/concatenate | solution.py:150
  232.5 2.9 reshape.454
  235.4 2.1 constant_dynamic-update-slice_fusion
  238.3 1.4 dynamic-update-slice.2
  239.7 2.1 copy.40
  241.8 5.7 %reshape.459 = bf16[1310720]{0:T(1024)(128)(2,1)} reshape(bf16[2048,640]{1,0:T(8,128)(2,1)} %convolution_convert_fusion) | data formatting | bytes 5242880 | tf_op jit(solution)/shard_map/reshape | solution.py:345
  251.0 44.6 %pad_maximum_fusion = bf16[3932160]{0:T(1024)(128)(2,1)} fusion(bf16[1310720]{0:T(1024)(128)(2,1)S(1)} %copy-done.5, bf16[1310720]{0:T(1024)(128)(2,1)S(1)} %bitcast.91, bf16[1310720]{0:T(1024)(128)(2,1)S(1)} %bitcast.92), kind=kLoop, calls=%fused_computation | loop fusion | flops 23592960 | bytes 15728640 | tf_op jit(solution)/shard_map/concatenate | solution.py:345
  297.5 215.1 %all-reduce.9.cloned.1.call-done = (bf16[1671168]{0:T(1024)(128)(2,1)}, bf16[3932160]{0:T(1024)(128)(2,1)}) async-done(((bf16[1671168]{0:T(1024)(128)(2,1)}, bf16[3932160]{0:T(1024)(128)(2,1)}), (bf16[1671168]{0:T(1024)(128)(2,1)}, bf16[3932160]{0:T(1024)(128)(2,1)})) %all-reduce.9.cloned.1.call-update) | async-done | bytes 11206672
  514.3 1.0 dynamic-slice.1
  515.3 1.7 multiply_subtract_fusion
  (248 shorter events, 30.8 us)
Async XLA Ops:
  7.2 66.7 %all-gather.3.cloned.1.call-start = ((), (), s32[]{:S(2)}) async-start(), calls=%async_computation | async-start | bytes 3446784 | tf_op jit(solution)/shard_map/all_gather | solution.py:336
  11.1 139.7 %all-gather.5.cloned.1.call-start = ((), (), s32[]{:S(2)}) async-start(), calls=%async_computation.1 | async-start | bytes 8110080 | tf_op jit(solution)/shard_map/all_gather | solution.py:339
  11.9 500.7 %all-reduce.9.cloned.1.call-start = ((), (), s32[]{:S(2)}) async-start(), calls=%async_computation.2 | async-start | bytes 22413312
  16.6 57.2 %copy-start.76 = (f32[128]{0:T(128)}, f32[128]{0:T(128)S(1)}, u32[]{:S(2)}) copy-start(f32[128]{0:T(128)S(1)} %fusion.32) | copy-start | bytes 1540
  16.6 81.0 %copy-start.51 = (f32[128]{0:T(128)}, f32[128]{0:T(128)S(1)}, u32[]{:S(2)}) copy-start(f32[128]{0:T(128)S(1)} %fusion.77) | copy-start | bytes 1540
  95.7 3.3 copy-start.69
  95.8 3.3 copy-start.71
  98.4 3.5 copy-start.59
  101.9 4.0 copy-start.37
  102.1 3.9 copy-start.18
  171.8 3.1 copy-start.11
  173.4 2.9 copy-start.13
  173.4 2.9 copy-start.73
  176.3 2.9 copy-start.20
  176.3 2.9 copy-start.22
  179.3 4.3 copy-start.19
  180.8 4.5 copy-start.38
  181.0 4.6 copy-start.17
  183.6 3.9 copy-start.47
  183.6 4.1 copy-start.42
  183.6 4.1 copy-start.44
  184.1 3.7 copy-start.50
  185.4 3.9 copy-start.55
  185.4 3.9 copy-start.60
  187.8 4.5 copy-start.53
  189.4 4.7 copy-start.66
  189.4 4.7 copy-start.74
  189.4 4.7 copy-start.79
  189.6 4.4 copy-start.12
  192.4 5.2 copy-start.21
  194.0 6.0 %copy-start.23 = (bf16[128,2048]{1,0:T(8,128)(2,1)S(1)}, bf16[128,2048]{1,0:T(8,128)(2,1)}, u32[]{:S(2)}) copy-start(bf16[128,2048]{1,0:T(8,128)(2,1)} %copy-done.22) | copy-start | bytes 1572868
  197.6 4.9 copy-start.31
  197.6 4.9 copy-start.34
  197.6 4.9 copy-start.36
  200.1 3.1 copy-start.29
  200.1 3.1 copy-start.57
  200.1 3.1 copy-start.68
  200.1 3.3 copy-start.81
  200.1 3.4 copy-start.45
  203.2 6.2 %copy-start.64 = (bf16[3072]{0:T(1024)(128)(2,1)S(1)}, bf16[3072]{0:T(1024)(128)(2,1)}, u32[]{:S(2)}) copy-start(bf16[3072]{0:T(1024)(128)(2,1)} %custom-call.1) | copy-start | bytes 18436
  203.2 6.4 %copy-start.75 = (bf16[256]{0:T(256)(128)(2,1)S(1)}, bf16[256]{0:T(256)(128)(2,1)}, u32[]{:S(2)}) copy-start(bf16[256]{0:T(256)(128)(2,1)} %get-tuple-element.6) | copy-start | bytes 1540
  203.2 6.8 %copy-start.63 = (bf16[640]{0:T(1024)(128)(2,1)S(1)}, bf16[640]{0:T(1024)(128)(2,1)}, u32[]{:S(2)}) copy-start(bf16[640]{0:T(1024)(128)(2,1)} %get-tuple-element.10) | copy-start | bytes 3844
  203.2 7.0 %copy-start.61 = (bf16[640]{0:T(1024)(128)(2,1)S(1)}, bf16[640]{0:T(1024)(128)(2,1)}, u32[]{:S(2)}) copy-start(bf16[640]{0:T(1024)(128)(2,1)} %get-tuple-element.8) | copy-start | bytes 3844
  203.2 7.2 %copy-start.62 = (bf16[640]{0:T(1024)(128)(2,1)S(1)}, bf16[640]{0:T(1024)(128)(2,1)}, u32[]{:S(2)}) copy-start(bf16[640]{0:T(1024)(128)(2,1)} %get-tuple-element.12) | copy-start | bytes 3844
  241.8 5.7 %copy-start.1 = (bf16[80,16,8,128]{3,2,1,0:T(8,128)(2,1)S(1)}, bf16[80,16,8,128]{3,2,1,0:T(8,128)(2,1)}, u32[]{:S(2)}) copy-start(bf16[80,16,8,128]{3,2,1,0:T(8,128)(2,1)} %fusion.1) | copy-start | bytes 7864324
  295.6 219.7 %copy-start.16 = (f32[174176]{0:T(1024)S(1)}, f32[174176]{0:T(1024)}, u32[]{:S(2)}) copy-start(f32[174176]{0:T(1024)} %param.9) | copy-start | bytes 2090116
  295.6 219.7 %copy-start.39 = (f32[174176]{0:T(1024)S(1)}, f32[174176]{0:T(1024)}, u32[]{:S(2)}) copy-start(f32[174176]{0:T(1024)} %param.10) | copy-start | bytes 2090116
  295.6 219.7 %copy-start.40 = (f32[174176]{0:T(1024)S(1)}, f32[174176]{0:T(1024)}, u32[]{:S(2)}) copy-start(f32[174176]{0:T(1024)} %param.11) | copy-start | bytes 2090116
  (37 other events, 60.9 us)
Sparse Core Ops, SparseCore 0:
  11.4 62.4 all-gather.2
  77.3 73.4 all-gather.4
  295.8 216.8 all-reduce.8
